TPU v7x, 128 devices: a whole 4x4x4 slice. The times are simulated.
128 devices in a mesh: grp: 8 (over y, core), dev: 16 (over z, x).
Axes of the slice: x: 4, y: 4, z: 4, core: 2. Of those that a mesh axis runs over, the one named last changes fastest.
Arguments:
- basis_old: float32 [128, 2097152], P(None, ('grp', 'dev')), as said below
- values_old: float32 [128], replicated, may hold values from 1 to 4
- snapshots: float32 [2, 64, 2097152], P(None, None, ('grp', 'dev'))
- wet_counts: int32 [128], P(('grp', 'dev')), may hold values from 1 to 128, as said below
Outputs:
- basis_new: float32 [128, 2097152], P(None, ('grp', 'dev'))
- values_new: float32 [128], replicated
Inputs may be any that keep to these rules, and one draw needn't show every extreme that they name: `wet_counts`: every device has at least one wet block, and some device has all 128 blocks wet. basis_old is zero on every cell that wet_mask marks dry.
All inputs are finite; a program needn't handle non-finite values.
Results may differ from a plain program's by a relative error of at most 0.0003.
Values sent between devices are 32-bit elements; how exact they have to be, the bound alone decides.
No kernel may reach another device: no remote copies, remote signals or barrier semaphores. Data moves between devices by JAX's collectives and lax.ppermute only.
A program may use at most 128 MiB of HBM per device.

v0:
```python
import jax
import jax.numpy as jnp
from jax import lax
from jax.sharding import PartitionSpec as P

BLOCK = 128
SWEEPS = 3


def matmul_nn(left_op, right_op):
    return jnp.dot(
        left_op, right_op, precision=lax.Precision.HIGHEST, preferred_element_type=jnp.float32
    )


def matmul_nt(left_op, right_op):
    return lax.dot_general(
        left_op,
        right_op,
        (((1,), (1,)), ((), ())),
        precision=lax.Precision.HIGHEST,
        preferred_element_type=jnp.float32,
    )


def matmul_tn(left_op, right_op):
    return lax.dot_general(
        left_op,
        right_op,
        (((0,), (0,)), ((), ())),
        precision=lax.Precision.HIGHEST,
        preferred_element_type=jnp.float32,
    )


def assemble(values, project, factor):
    upper_block = jnp.concatenate([jnp.diag(values), project], 1)
    bottom = jnp.concatenate(
        [jnp.zeros((factor.shape[0], values.shape[0]), jnp.float32), factor.T], 1
    )
    return jnp.concatenate([upper_block, bottom], 0)


def refine(core_matrix, rank_width):
    frame_now = jnp.eye(core_matrix.shape[0], rank_width, dtype=jnp.float32)
    for repeat in range(SWEEPS):
        grown_cols = matmul_nn(core_matrix, matmul_tn(core_matrix, frame_now))
        lower_part = jnp.linalg.cholesky(matmul_tn(grown_cols, grown_cols))
        frame_now = jax.scipy.linalg.solve_triangular(lower_part, grown_cols.T, lower=True).T
    return frame_now


def per_device(basis_old, values_old, snapshots, wet_counts):
    counts = lax.all_gather(wet_counts, ("grp", "dev"), axis=0, tiled=True)
    wet_total = jnp.sum(counts).astype(jnp.float32) * BLOCK
    rows_here = basis_old.shape[1]
    wet_mask = (lax.iota(jnp.int32, rows_here) // BLOCK < wet_counts[0]).astype(jnp.float32)
    rank_width = basis_old.shape[0]

    def update_one(state_pair, snapshot):
        current, values = state_pair
        columns = snapshot * wet_mask[None, :]
        project = lax.psum(matmul_nt(current, columns), ("grp", "dev")) / wet_total
        remainder = columns - matmul_tn(project, current)
        gram = lax.psum(matmul_nt(remainder, remainder), ("grp", "dev")) / wet_total
        factor = jnp.linalg.cholesky(gram)
        fresh_rows = jax.scipy.linalg.solve_triangular(factor, remainder, lower=True)
        core_matrix = assemble(values, project, factor)
        frame_now = refine(core_matrix, rank_width)
        stacked = jnp.concatenate([current, fresh_rows], 0)
        new_basis = matmul_tn(frame_now, stacked)
        rotated = matmul_tn(frame_now, core_matrix)
        new_values = jnp.sqrt(jnp.sum(rotated * rotated, axis=1))
        return ((new_basis, new_values), None)

    (current, values), _ = lax.scan(update_one, (basis_old, values_old), snapshots)
    return (current, values)


def solution(mesh):
    return jax.shard_map(
        per_device,
        mesh=mesh,
        in_specs=(P(None, ("grp", "dev")), P(), P(None, None, ("grp", "dev")), P(("grp", "dev"))),
        out_specs=(P(None, ("grp", "dev")), P()),
        check_vma=False,
    )
```

profile of v0, /device:TPU:1, one launch (start us, length us, event | category | flops | bytes accessed | tf_op | source)
XLA Modules:
  0.0 607.9 jit_solution(14972124603921048518)
XLA Ops:
  0.6 7.6 %copy.42 = f32[128,16384]{1,0:T(8,128)} copy(f32[128,16384]{1,0:T(8,128)} %param.9) | data formatting | bytes 16777216
  9.0 68.6 %all-reduce.1 = s32[128]{0:T(128)S(1)} all-reduce(s32[128]{0:T(128)S(1)} %dynamic-update-slice.5), channel_id=1, replica_groups=mesh['grp'=8,'dev'=16] {'grp','dev'}, use_global_device_ids=true, to_apply=%add.1 | all-reduce | flops 128 | bytes 1024
  77.6 0.7 reduce_sum.18
  79.0 527.8 %while.13 = (s32[]{:T(128)}, f32[128,16384]{1,0:T(8,128)}, f32[128]{0:T(128)S(1)}, f32[2,64,16384]{2,1,0:T(8,128)}, f32[]{:T(128)}, /*index=5*/s32[]{:T(128)}, s32[]{:T(128)}) while((s32[]{:T(128)}, f32[128,16384]{1,0:T(8,128)}, f32[128]{0:T(128)S(1)}, f32[2,64,16384]{2,1,0:T(8,128)}, f32[]{:T(128)}, /*index=5*/s32[]{:T(128)}, ...), condition=%wide.region_9.12_spmd.clone, body=%wide.region_1.11_spmd.clone.sunk | while | flops 10294632448 | bytes 169318064 | solution.py:76
  79.3 3.5 copy.45
  82.8 1.6 fusion.152
  84.4 2.7 copy-done
  87.1 1.0 copy-done.2
  88.1 8.8 %fusion.153 = f32[128,64]{0,1:T(8,128)S(1)} fusion(f32[128,16384]{1,0:T(8,128)S(1)} %copy.45, f32[2,64,16384]{2,1,0:T(8,128)S(1)} %copy-done.2, s32[]{:T(128)} %get-tuple-element.116, f32[16384]{0:T(1024)S(1)} %fusion.152), kind=kOutput, calls=%fused_computation.11.clone.1 | convolution fusion | flops 1611661312 | bytes 12681220 | tf_op jit(solution)/shard_map/while/body/eval_jaxpr/dot_general | solution.py:17
  96.9 62.9 %psum.18 = f32[128,64]{0,1:T(8,128)S(1)} all-reduce(f32[128,64]{0,1:T(8,128)S(1)} %fusion.153), channel_id=1, replica_groups=mesh['grp'=8,'dev'=16] {'grp','dev'}, use_global_device_ids=true, to_apply=%region_2.2 | all-reduce | flops 8192 | bytes 65536 | tf_op jit(solution)/shard_map/while/body/eval_jaxpr/psum | solution.py:63
  159.8 7.8 %convolution_subtract_fusion.2 = f32[64,16384]{1,0:T(8,128)S(1)} fusion(f32[128,64]{0,1:T(8,128)S(1)} %broadcast_divide_fusion.4, f32[128,16384]{1,0:T(8,128)} %copy-done, f32[2,64,16384]{2,1,0:T(8,128)} %get-tuple-element.126, s32[]{:T(128)} %get-tuple-element.116, f32[16384]{0:T(1024)S(1)} %fusion.152), kind=kOutput, calls=%fused_computation.1.clone.1 | convolution fusion | flops 1612709888 | bytes 16875524 | tf_op jit(solution)/shard_map/while/body/eval_jaxpr/dot_general | solution.py:27
  167.6 2.0 copy-done.1
  169.6 3.4 fusion.154
  173.0 64.8 %psum.19 = f32[64,64]{0,1:T(8,128)S(1)} all-reduce(f32[64,64]{0,1:T(8,128)S(1)} %fusion.154), channel_id=1, replica_groups=mesh['grp'=8,'dev'=16] {'grp','dev'}, use_global_device_ids=true, to_apply=%region_3.3 | all-reduce | flops 4096 | bytes 32768 | tf_op jit(solution)/shard_map/while/body/eval_jaxpr/psum | solution.py:65
  238.0 5.8 cholesky.285
  243.9 0.7 compare_reduce_fusion.8
  246.7 11.7 %cholesky.286 = f32[128,128]{1,0:T(8,128)S(1)} custom-call(f32[128,128]{1,0:T(8,128)S(1)} %fusion.160), custom_call_target="Cholesky" | custom-call | tf_op jit(solution)/shard_map/while/body/eval_jaxpr/jit(cholesky)/cholesky | solution.py:48
  258.4 0.7 compare_reduce_fusion.9
  259.7 9.8 %custom-call.22 = f32[1,128,128]{1,2,0:T(8,128)S(1)} custom-call(f32[1,128,128]{2,1,0:T(8,128)S(1)} %fusion.162), custom_call_target="InvertDiagBlocksLowerTriangular" | custom-call | tf_op jit(solution)/shard_map/while/body/eval_jaxpr/jit(_solve_triangular)/triangular_solve | solution.py:49
  271.3 11.9 %cholesky.287 = f32[128,128]{1,0:T(8,128)S(1)} custom-call(f32[128,128]{1,0:T(8,128)S(1)} %fusion.167), custom_call_target="Cholesky" | custom-call | tf_op jit(solution)/shard_map/while/body/eval_jaxpr/jit(cholesky)/cholesky | solution.py:48
  284.5 9.8 %custom-call.23 = f32[1,128,128]{1,2,0:T(8,128)S(1)} custom-call(f32[1,128,128]{2,1,0:T(8,128)S(1)} %fusion.169), custom_call_target="InvertDiagBlocksLowerTriangular" | custom-call | tf_op jit(solution)/shard_map/while/body/eval_jaxpr/jit(_solve_triangular)/triangular_solve | solution.py:49
  296.0 11.7 %cholesky.288 = f32[128,128]{1,0:T(8,128)S(1)} custom-call(f32[128,128]{1,0:T(8,128)S(1)} %fusion.174), custom_call_target="Cholesky" | custom-call | tf_op jit(solution)/shard_map/while/body/eval_jaxpr/jit(cholesky)/cholesky | solution.py:48
  307.8 0.7 compare_reduce_fusion.11
  309.1 9.8 %custom-call.24 = f32[1,128,128]{1,2,0:T(8,128)S(1)} custom-call(f32[1,128,128]{2,1,0:T(8,128)S(1)} %fusion.175), custom_call_target="InvertDiagBlocksLowerTriangular" | custom-call | tf_op jit(solution)/shard_map/while/body/eval_jaxpr/jit(_solve_triangular)/triangular_solve | solution.py:49
  319.7 4.9 custom-call.25
  324.6 5.6 fusion.177
  330.2 12.3 %fusion.178 = f32[128,16384]{1,0:T(8,128)} fusion(f32[128,192]{0,1:T(8,128)S(1)} %fusion.176, f32[64,16384]{1,0:T(8,128)S(1)} %fusion.177, f32[128,16384]{1,0:T(8,128)} %copy-done), kind=kOutput, calls=%fused_computation.2.clone.1 | convolution fusion | flops 4834983936 | bytes 21069824 | tf_op jit(solution)/shard_map/while/body/eval_jaxpr/dot_general | solution.py:27
  342.8 3.5 copy.45
  346.3 1.6 fusion.152
  347.9 2.7 copy-done
  350.6 1.0 copy-done.2
  351.6 8.8 %fusion.153 = f32[128,64]{0,1:T(8,128)S(1)} fusion(f32[128,16384]{1,0:T(8,128)S(1)} %copy.45, f32[2,64,16384]{2,1,0:T(8,128)S(1)} %copy-done.2, s32[]{:T(128)} %get-tuple-element.116, f32[16384]{0:T(1024)S(1)} %fusion.152), kind=kOutput, calls=%fused_computation.11.clone.1 | convolution fusion | flops 1611661312 | bytes 12681220 | tf_op jit(solution)/shard_map/while/body/eval_jaxpr/dot_general | solution.py:17
  360.4 63.0 %psum.18 = f32[128,64]{0,1:T(8,128)S(1)} all-reduce(f32[128,64]{0,1:T(8,128)S(1)} %fusion.153), channel_id=1, replica_groups=mesh['grp'=8,'dev'=16] {'grp','dev'}, use_global_device_ids=true, to_apply=%region_2.2 | all-reduce | flops 8192 | bytes 65536 | tf_op jit(solution)/shard_map/while/body/eval_jaxpr/psum | solution.py:63
  423.4 7.8 %convolution_subtract_fusion.2 = f32[64,16384]{1,0:T(8,128)S(1)} fusion(f32[128,64]{0,1:T(8,128)S(1)} %broadcast_divide_fusion.4, f32[128,16384]{1,0:T(8,128)} %copy-done, f32[2,64,16384]{2,1,0:T(8,128)} %get-tuple-element.126, s32[]{:T(128)} %get-tuple-element.116, f32[16384]{0:T(1024)S(1)} %fusion.152), kind=kOutput, calls=%fused_computation.1.clone.1 | convolution fusion | flops 1612709888 | bytes 16875524 | tf_op jit(solution)/shard_map/while/body/eval_jaxpr/dot_general | solution.py:27
  431.2 2.0 copy-done.1
  433.2 3.4 fusion.154
  436.6 64.4 %psum.19 = f32[64,64]{0,1:T(8,128)S(1)} all-reduce(f32[64,64]{0,1:T(8,128)S(1)} %fusion.154), channel_id=1, replica_groups=mesh['grp'=8,'dev'=16] {'grp','dev'}, use_global_device_ids=true, to_apply=%region_3.3 | all-reduce | flops 4096 | bytes 32768 | tf_op jit(solution)/shard_map/while/body/eval_jaxpr/psum | solution.py:65
  501.1 5.8 cholesky.285
  507.0 0.7 compare_reduce_fusion.8
  509.8 11.7 %cholesky.286 = f32[128,128]{1,0:T(8,128)S(1)} custom-call(f32[128,128]{1,0:T(8,128)S(1)} %fusion.160), custom_call_target="Cholesky" | custom-call | tf_op jit(solution)/shard_map/while/body/eval_jaxpr/jit(cholesky)/cholesky | solution.py:48
  522.8 9.8 %custom-call.22 = f32[1,128,128]{1,2,0:T(8,128)S(1)} custom-call(f32[1,128,128]{2,1,0:T(8,128)S(1)} %fusion.162), custom_call_target="InvertDiagBlocksLowerTriangular" | custom-call | tf_op jit(solution)/shard_map/while/body/eval_jaxpr/jit(_solve_triangular)/triangular_solve | solution.py:49
  534.4 11.9 %cholesky.287 = f32[128,128]{1,0:T(8,128)S(1)} custom-call(f32[128,128]{1,0:T(8,128)S(1)} %fusion.167), custom_call_target="Cholesky" | custom-call | tf_op jit(solution)/shard_map/while/body/eval_jaxpr/jit(cholesky)/cholesky | solution.py:48
  547.6 9.8 %custom-call.23 = f32[1,128,128]{1,2,0:T(8,128)S(1)} custom-call(f32[1,128,128]{2,1,0:T(8,128)S(1)} %fusion.169), custom_call_target="InvertDiagBlocksLowerTriangular" | custom-call | tf_op jit(solution)/shard_map/while/body/eval_jaxpr/jit(_solve_triangular)/triangular_solve | solution.py:49
  559.2 11.7 %cholesky.288 = f32[128,128]{1,0:T(8,128)S(1)} custom-call(f32[128,128]{1,0:T(8,128)S(1)} %fusion.174), custom_call_target="Cholesky" | custom-call | tf_op jit(solution)/shard_map/while/body/eval_jaxpr/jit(cholesky)/cholesky | solution.py:48
  572.3 9.8 %custom-call.24 = f32[1,128,128]{1,2,0:T(8,128)S(1)} custom-call(f32[1,128,128]{2,1,0:T(8,128)S(1)} %fusion.175), custom_call_target="InvertDiagBlocksLowerTriangular" | custom-call | tf_op jit(solution)/shard_map/while/body/eval_jaxpr/jit(_solve_triangular)/triangular_solve | solution.py:49
  582.8 4.9 custom-call.25
  587.7 5.8 fusion.177
  593.6 12.3 %fusion.178 = f32[128,16384]{1,0:T(8,128)} fusion(f32[128,192]{0,1:T(8,128)S(1)} %fusion.176, f32[64,16384]{1,0:T(8,128)S(1)} %fusion.177, f32[128,16384]{1,0:T(8,128)} %copy-done), kind=kOutput, calls=%fused_computation.2.clone.1 | convolution fusion | flops 4834983936 | bytes 21069824 | tf_op jit(solution)/shard_map/while/body/eval_jaxpr/dot_general | solution.py:27
  (86 shorter events, 20.0 us)
Async XLA Ops:
  0.6 78.4 %copy-start.4 = (f32[128]{0:T(128)S(1)}, f32[128]{0:T(128)}, u32[]{:S(2)}) copy-start(f32[128]{0:T(128)} %param.10) | copy-start | bytes 1540
  79.3 8.8 %copy-start.2 = (f32[2,64,16384]{2,1,0:T(8,128)S(1)}, f32[2,64,16384]{2,1,0:T(8,128)}, u32[]{:S(2)}) copy-start(f32[2,64,16384]{2,1,0:T(8,128)} %get-tuple-element.126) | copy-start | bytes 25165828 | tf_op jit(solution)/shard_map/while
  82.8 4.3 copy-start
  167.6 2.0 copy-start.1
  342.8 8.8 %copy-start.2 = (f32[2,64,16384]{2,1,0:T(8,128)S(1)}, f32[2,64,16384]{2,1,0:T(8,128)}, u32[]{:S(2)}) copy-start(f32[2,64,16384]{2,1,0:T(8,128)} %get-tuple-element.126) | copy-start | bytes 25165828 | tf_op jit(solution)/shard_map/while
  346.3 4.3 copy-start
  431.2 2.0 copy-start.1
  606.9 0.5 copy-start.3
where the time goes:
time: 611 us; the launch traced here: 608 us
  blocking collectives  324 us (53%)
  other arithmetic  166 us (27%)
  matrix products  86 us (14%)
  local copies, waits for them, and re-layouts  27.7 us (5%)
    psum x2, blocking collectives, update_one(): gram = lax.psum(matmul_nt(remainder, remainder), ('grp', 'dev')) / wet_total  129 us
    psum x2, blocking collectives, update_one(): project = lax.psum(matmul_nt(current, columns), ('grp', 'dev')) / wet_total  126 us
    another operation x18, other arithmetic, refine(): lower_part = jnp.linalg.cholesky(matmul_tn(grown_cols, grown_cols))  74.8 us
    unnamed x1, blocking collectives  68.6 us
    another operation x12, other arithmetic, refine(): jax.scipy.linalg.solve_triangular(lower_part, grown_cols.T, lower=True)  62.7 us
    dot_general x18, matrix products, matmul_tn(): lax.dot_general(left_op, right_op, (((0,), (0,)), ((), ())), precision=la...  46.3 us
    dot_general x4, matrix products, matmul_nt(): lax.dot_general(left_op, right_op, (((1,), (1,)), ((), ())), precision=la...  24.4 us
    while x16, local copies, waits for them, and re-layouts  18.6 us

commit v1 on v0

--- a/solution.py
+++ b/solution.py
@@ -5,6 +5,11 @@
 
 BLOCK = 128
 SWEEPS = 3
+
+
+def axis_by_axis(value, axis_one, axis_two):
+    inner = lax.psum(value, axis_one)
+    return lax.psum(inner, axis_two)
 
 
 def matmul_nn(left_op, right_op):
@@ -62,7 +67,7 @@
         columns = snapshot * wet_mask[None, :]
         project = lax.psum(matmul_nt(current, columns), ("grp", "dev")) / wet_total
         remainder = columns - matmul_tn(project, current)
-        gram = lax.psum(matmul_nt(remainder, remainder), ("grp", "dev")) / wet_total
+        gram = axis_by_axis(matmul_nt(remainder, remainder), "grp", "dev") / wet_total
         factor = jnp.linalg.cholesky(gram)
         fresh_rows = jax.scipy.linalg.solve_triangular(factor, remainder, lower=True)
         core_matrix = assemble(values, project, factor)

time: 611 us -> 673 us (1.10)
  the two profiles are of different devices: /device:TPU:1 before, /device:TPU:0 now
where the time goes in v1:
time: 673 us; the launch traced here: 670 us
  blocking collectives  386 us (57%)
  other arithmetic  166 us (25%)
  matrix products  86.1 us (13%)
  local copies, waits for them, and re-layouts  27.7 us (4%)
    psum x2, blocking collectives, axis_by_axis(): return lax.psum(inner, axis_two)  143 us
    psum x2, blocking collectives, update_one(): project = lax.psum(matmul_nt(current, columns), ('grp', 'dev')) / wet_total  126 us
    another operation x18, other arithmetic, refine(): lower_part = jnp.linalg.cholesky(matmul_tn(grown_cols, grown_cols))  74.8 us
    unnamed x1, blocking collectives  68.2 us
    another operation x12, other arithmetic, refine(): jax.scipy.linalg.solve_triangular(lower_part, grown_cols.T, lower=True)  62.7 us
    psum x2, blocking collectives, axis_by_axis(): inner = lax.psum(value, axis_one)  48.9 us
    dot_general x18, matrix products, matmul_tn(): lax.dot_general(left_op, right_op, (((0,), (0,)), ((), ())), precision=la...  46.4 us
    dot_general x4, matrix products, matmul_nt(): lax.dot_general(left_op, right_op, (((1,), (1,)), ((), ())), precision=la...  24.4 us

profile of v1, /device:TPU:0, one launch (start us, length us, event | category | flops | bytes accessed | tf_op | source)
XLA Modules:
  0.0 670.1 jit_solution(5607160687362473600)
XLA Ops:
  0.6 7.6 %copy.42 = f32[128,16384]{1,0:T(8,128)} copy(f32[128,16384]{1,0:T(8,128)} %param.9) | data formatting | bytes 16777216
  9.0 68.2 %all-reduce.1 = s32[128]{0:T(128)S(1)} all-reduce(s32[128]{0:T(128)S(1)} %dynamic-update-slice.5), channel_id=1, replica_groups=mesh['grp'=8,'dev'=16] {'grp','dev'}, use_global_device_ids=true, to_apply=%add.1 | all-reduce | flops 128 | bytes 1024
  77.1 0.7 reduce_sum.18
  78.6 590.4 %while.13 = (s32[]{:T(128)}, f32[128,16384]{1,0:T(8,128)}, f32[128]{0:T(128)S(1)}, f32[2,64,16384]{2,1,0:T(8,128)}, f32[]{:T(128)}, /*index=5*/s32[]{:T(128)}, s32[]{:T(128)}) while((s32[]{:T(128)}, f32[128,16384]{1,0:T(8,128)}, f32[128]{0:T(128)S(1)}, f32[2,64,16384]{2,1,0:T(8,128)}, f32[]{:T(128)}, /*index=5*/s32[]{:T(128)}, ...), condition=%wide.region_10.13_spmd.clone, body=%wide.region_1.12_spmd.clone.sunk | while | flops 10294636544 | bytes 169350832 | solution.py:81
  78.8 3.5 copy.45
  82.4 1.6 fusion.152
  83.9 2.7 copy-done
  86.6 1.0 copy-done.2
  87.6 8.8 %fusion.153 = f32[128,64]{0,1:T(8,128)S(1)} fusion(f32[128,16384]{1,0:T(8,128)S(1)} %copy.45, f32[2,64,16384]{2,1,0:T(8,128)S(1)} %copy-done.2, s32[]{:T(128)} %get-tuple-element.116, f32[16384]{0:T(1024)S(1)} %fusion.152), kind=kOutput, calls=%fused_computation.11.clone.1 | convolution fusion | flops 1611661312 | bytes 12681220 | tf_op jit(solution)/shard_map/while/body/eval_jaxpr/dot_general | solution.py:22
  96.4 62.6 %psum.27 = f32[128,64]{0,1:T(8,128)S(1)} all-reduce(f32[128,64]{0,1:T(8,128)S(1)} %fusion.153), channel_id=1, replica_groups=mesh['grp'=8,'dev'=16] {'grp','dev'}, use_global_device_ids=true, to_apply=%region_2.2 | all-reduce | flops 8192 | bytes 65536 | tf_op jit(solution)/shard_map/while/body/eval_jaxpr/psum | solution.py:68
  159.0 7.8 %convolution_subtract_fusion.2 = f32[64,16384]{1,0:T(8,128)S(1)} fusion(f32[128,64]{0,1:T(8,128)S(1)} %broadcast_divide_fusion.4, f32[128,16384]{1,0:T(8,128)} %copy-done, f32[2,64,16384]{2,1,0:T(8,128)} %get-tuple-element.126, s32[]{:T(128)} %get-tuple-element.116, f32[16384]{0:T(1024)S(1)} %fusion.152), kind=kOutput, calls=%fused_computation.1.clone.1 | convolution fusion | flops 1612709888 | bytes 16875524 | tf_op jit(solution)/shard_map/while/body/eval_jaxpr/dot_general | solution.py:32
  166.8 2.0 copy-done.1
  168.8 3.4 fusion.154
  172.2 25.3 %psum.28 = f32[64,64]{0,1:T(8,128)S(1)} all-reduce(f32[64,64]{0,1:T(8,128)S(1)} %fusion.154), channel_id=1, replica_groups=mesh['grp'=8,'dev'=16] {'grp'}, use_global_device_ids=true, to_apply=%region_3.3 | all-reduce | flops 4096 | bytes 32768 | tf_op jit(solution)/shard_map/while/body/eval_jaxpr/psum | solution.py:11
  197.6 71.4 %psum.29 = f32[64,64]{0,1:T(8,128)S(1)} all-reduce(f32[64,64]{0,1:T(8,128)S(1)} %psum.28), channel_id=1, replica_groups=mesh['grp'=8,'dev'=16] {'dev'}, use_global_device_ids=true, to_apply=%region_4.4 | all-reduce | flops 4096 | bytes 32768 | tf_op jit(solution)/shard_map/while/body/eval_jaxpr/psum | solution.py:12
  269.1 5.8 cholesky.285
  275.0 0.7 compare_reduce_fusion.8
  277.7 11.7 %cholesky.286 = f32[128,128]{1,0:T(8,128)S(1)} custom-call(f32[128,128]{1,0:T(8,128)S(1)} %fusion.160), custom_call_target="Cholesky" | custom-call | tf_op jit(solution)/shard_map/while/body/eval_jaxpr/jit(cholesky)/cholesky | solution.py:53
  290.8 9.8 %custom-call.22 = f32[1,128,128]{1,2,0:T(8,128)S(1)} custom-call(f32[1,128,128]{2,1,0:T(8,128)S(1)} %fusion.162), custom_call_target="InvertDiagBlocksLowerTriangular" | custom-call | tf_op jit(solution)/shard_map/while/body/eval_jaxpr/jit(_solve_triangular)/triangular_solve | solution.py:54
  302.3 11.9 %cholesky.287 = f32[128,128]{1,0:T(8,128)S(1)} custom-call(f32[128,128]{1,0:T(8,128)S(1)} %fusion.167), custom_call_target="Cholesky" | custom-call | tf_op jit(solution)/shard_map/while/body/eval_jaxpr/jit(cholesky)/cholesky | solution.py:53
  315.6 9.8 %custom-call.23 = f32[1,128,128]{1,2,0:T(8,128)S(1)} custom-call(f32[1,128,128]{2,1,0:T(8,128)S(1)} %fusion.169), custom_call_target="InvertDiagBlocksLowerTriangular" | custom-call | tf_op jit(solution)/shard_map/while/body/eval_jaxpr/jit(_solve_triangular)/triangular_solve | solution.py:54
  327.1 11.7 %cholesky.288 = f32[128,128]{1,0:T(8,128)S(1)} custom-call(f32[128,128]{1,0:T(8,128)S(1)} %fusion.174), custom_call_target="Cholesky" | custom-call | tf_op jit(solution)/shard_map/while/body/eval_jaxpr/jit(cholesky)/cholesky | solution.py:53
  340.2 9.8 %custom-call.24 = f32[1,128,128]{1,2,0:T(8,128)S(1)} custom-call(f32[1,128,128]{2,1,0:T(8,128)S(1)} %fusion.175), custom_call_target="InvertDiagBlocksLowerTriangular" | custom-call | tf_op jit(solution)/shard_map/while/body/eval_jaxpr/jit(_solve_triangular)/triangular_solve | solution.py:54
  350.8 4.9 custom-call.25
  355.7 5.6 fusion.177
  361.3 12.3 %fusion.178 = f32[128,16384]{1,0:T(8,128)} fusion(f32[128,192]{0,1:T(8,128)S(1)} %fusion.176, f32[64,16384]{1,0:T(8,128)S(1)} %fusion.177, f32[128,16384]{1,0:T(8,128)} %copy-done), kind=kOutput, calls=%fused_computation.2.clone.1 | convolution fusion | flops 4834983936 | bytes 21069824 | tf_op jit(solution)/shard_map/while/body/eval_jaxpr/dot_general | solution.py:32
  373.9 3.5 copy.45
  377.4 1.6 fusion.152
  379.0 2.7 copy-done
  381.7 1.0 copy-done.2
  382.7 8.8 %fusion.153 = f32[128,64]{0,1:T(8,128)S(1)} fusion(f32[128,16384]{1,0:T(8,128)S(1)} %copy.45, f32[2,64,16384]{2,1,0:T(8,128)S(1)} %copy-done.2, s32[]{:T(128)} %get-tuple-element.116, f32[16384]{0:T(1024)S(1)} %fusion.152), kind=kOutput, calls=%fused_computation.11.clone.1 | convolution fusion | flops 1611661312 | bytes 12681220 | tf_op jit(solution)/shard_map/while/body/eval_jaxpr/dot_general | solution.py:22
  391.4 63.1 %psum.27 = f32[128,64]{0,1:T(8,128)S(1)} all-reduce(f32[128,64]{0,1:T(8,128)S(1)} %fusion.153), channel_id=1, replica_groups=mesh['grp'=8,'dev'=16] {'grp','dev'}, use_global_device_ids=true, to_apply=%region_2.2 | all-reduce | flops 8192 | bytes 65536 | tf_op jit(solution)/shard_map/while/body/eval_jaxpr/psum | solution.py:68
  454.6 7.8 %convolution_subtract_fusion.2 = f32[64,16384]{1,0:T(8,128)S(1)} fusion(f32[128,64]{0,1:T(8,128)S(1)} %broadcast_divide_fusion.4, f32[128,16384]{1,0:T(8,128)} %copy-done, f32[2,64,16384]{2,1,0:T(8,128)} %get-tuple-element.126, s32[]{:T(128)} %get-tuple-element.116, f32[16384]{0:T(1024)S(1)} %fusion.152), kind=kOutput, calls=%fused_computation.1.clone.1 | convolution fusion | flops 1612709888 | bytes 16875524 | tf_op jit(solution)/shard_map/while/body/eval_jaxpr/dot_general | solution.py:32
  462.4 2.0 copy-done.1
  464.4 3.4 fusion.154
  467.8 23.6 %psum.28 = f32[64,64]{0,1:T(8,128)S(1)} all-reduce(f32[64,64]{0,1:T(8,128)S(1)} %fusion.154), channel_id=1, replica_groups=mesh['grp'=8,'dev'=16] {'grp'}, use_global_device_ids=true, to_apply=%region_3.3 | all-reduce | flops 4096 | bytes 32768 | tf_op jit(solution)/shard_map/while/body/eval_jaxpr/psum | solution.py:11
  491.4 71.7 %psum.29 = f32[64,64]{0,1:T(8,128)S(1)} all-reduce(f32[64,64]{0,1:T(8,128)S(1)} %psum.28), channel_id=1, replica_groups=mesh['grp'=8,'dev'=16] {'dev'}, use_global_device_ids=true, to_apply=%region_4.4 | all-reduce | flops 4096 | bytes 32768 | tf_op jit(solution)/shard_map/while/body/eval_jaxpr/psum | solution.py:12
  563.3 5.8 cholesky.285
  569.2 0.7 compare_reduce_fusion.8
  571.9 11.7 %cholesky.286 = f32[128,128]{1,0:T(8,128)S(1)} custom-call(f32[128,128]{1,0:T(8,128)S(1)} %fusion.160), custom_call_target="Cholesky" | custom-call | tf_op jit(solution)/shard_map/while/body/eval_jaxpr/jit(cholesky)/cholesky | solution.py:53
  585.0 9.8 %custom-call.22 = f32[1,128,128]{1,2,0:T(8,128)S(1)} custom-call(f32[1,128,128]{2,1,0:T(8,128)S(1)} %fusion.162), custom_call_target="InvertDiagBlocksLowerTriangular" | custom-call | tf_op jit(solution)/shard_map/while/body/eval_jaxpr/jit(_solve_triangular)/triangular_solve | solution.py:54
  596.5 11.9 %cholesky.287 = f32[128,128]{1,0:T(8,128)S(1)} custom-call(f32[128,128]{1,0:T(8,128)S(1)} %fusion.167), custom_call_target="Cholesky" | custom-call | tf_op jit(solution)/shard_map/while/body/eval_jaxpr/jit(cholesky)/cholesky | solution.py:53
  609.8 9.8 %custom-call.23 = f32[1,128,128]{1,2,0:T(8,128)S(1)} custom-call(f32[1,128,128]{2,1,0:T(8,128)S(1)} %fusion.169), custom_call_target="InvertDiagBlocksLowerTriangular" | custom-call | tf_op jit(solution)/shard_map/while/body/eval_jaxpr/jit(_solve_triangular)/triangular_solve | solution.py:54
  621.3 11.7 %cholesky.288 = f32[128,128]{1,0:T(8,128)S(1)} custom-call(f32[128,128]{1,0:T(8,128)S(1)} %fusion.174), custom_call_target="Cholesky" | custom-call | tf_op jit(solution)/shard_map/while/body/eval_jaxpr/jit(cholesky)/cholesky | solution.py:53
  634.4 9.8 %custom-call.24 = f32[1,128,128]{1,2,0:T(8,128)S(1)} custom-call(f32[1,128,128]{2,1,0:T(8,128)S(1)} %fusion.175), custom_call_target="InvertDiagBlocksLowerTriangular" | custom-call | tf_op jit(solution)/shard_map/while/body/eval_jaxpr/jit(_solve_triangular)/triangular_solve | solution.py:54
  645.0 4.9 custom-call.25
  649.9 5.8 fusion.177
  655.7 12.3 %fusion.178 = f32[128,16384]{1,0:T(8,128)} fusion(f32[128,192]{0,1:T(8,128)S(1)} %fusion.176, f32[64,16384]{1,0:T(8,128)S(1)} %fusion.177, f32[128,16384]{1,0:T(8,128)} %copy-done), kind=kOutput, calls=%fused_computation.2.clone.1 | convolution fusion | flops 4834983936 | bytes 21069824 | tf_op jit(solution)/shard_map/while/body/eval_jaxpr/dot_general | solution.py:32
  (88 shorter events, 21.3 us)
Async XLA Ops:
  0.6 77.9 %copy-start.4 = (f32[128]{0:T(128)S(1)}, f32[128]{0:T(128)}, u32[]{:S(2)}) copy-start(f32[128]{0:T(128)} %param.10) | copy-start | bytes 1540
  78.8 8.8 %copy-start.2 = (f32[2,64,16384]{2,1,0:T(8,128)S(1)}, f32[2,64,16384]{2,1,0:T(8,128)}, u32[]{:S(2)}) copy-start(f32[2,64,16384]{2,1,0:T(8,128)} %get-tuple-element.126) | copy-start | bytes 25165828 | tf_op jit(solution)/shard_map/while
  82.4 4.3 copy-start
  166.8 2.0 copy-start.1
  373.9 8.8 %copy-start.2 = (f32[2,64,16384]{2,1,0:T(8,128)S(1)}, f32[2,64,16384]{2,1,0:T(8,128)}, u32[]{:S(2)}) copy-start(f32[2,64,16384]{2,1,0:T(8,128)} %get-tuple-element.126) | copy-start | bytes 25165828 | tf_op jit(solution)/shard_map/while
  377.4 4.3 copy-start
  462.4 2.0 copy-start.1
  669.0 0.5 copy-start.3
